TPU v7x, 32 devices: a whole 2x2x4 slice. The times are simulated.
32 devices in a mesh: dp: 2 (over x), row: 4 (over y, core), col: 4 (over z).
Axes of the slice: x: 2, y: 2, z: 4, core: 2. Of those that a mesh axis runs over, the one named last changes fastest.
Arguments:
- tokens: bfloat16 [5120, 2048], P(('dp', 'col'), 'row'), may hold values from -6 to 6
- cotangent: bfloat16 [5120, 2048], P(('dp', 'col'), 'row'), may hold values from -6 to 6
- seg_ids: int32 [5120], P('dp'), may hold values from 0 to 12, as said below
- positions: int32 [5120], P('dp'), may hold values from 0 to 1279, as said below
- parents: int32 [2, 13], P('dp'), may hold values from 0 to 4, as said below
- tree_sets: int32 [2], P('dp'), may hold values from 0 to 7
- gain_q: float32 [2048], P('col'), may hold values from 0.25 to 1.75
- gain_k: float32 [2048], P('col'), may hold values from 0.25 to 1.75
- gain_attn: float32 [2048], P('row'), may hold values from 0.25 to 1.75
- gain_ffn: float32 [2048], P('row'), may hold values from 0.25 to 1.75
- query_key_value_weight: bfloat16 [2048, 3, 2048], P('row', None, 'col'), may hold values from -0.125 to 0.125
- output_weight: bfloat16 [2048, 2048], P('col', 'row'), may hold values from -0.125 to 0.125
- gate_up_weight: bfloat16 [2048, 2, 8192], P('row', None, 'col'), may hold values from -0.125 to 0.125
- down_weight: bfloat16 [8192, 2048], P('col', 'row'), may hold values from -0.0625 to 0.0625
- query_key_value_adapter_first: float32 [3, 8, 16, 2048], P(None, None, None, 'row'), may hold values from -0.125 to 0.125
- query_key_value_adapter_second: float32 [3, 8, 16, 2048], P(None, None, None, 'col'), may hold values from -0.5 to 0.5
- output_adapter_first: float32 [8, 16, 2048], P(None, None, 'col'), may hold values from -0.125 to 0.125
- output_adapter_second: float32 [8, 16, 2048], P(None, None, 'row'), may hold values from -0.5 to 0.5
- gate_up_adapter_first: float32 [2, 8, 16, 2048], P(None, None, None, 'row'), may hold values from -0.125 to 0.125
- gate_up_adapter_second: float32 [2, 8, 16, 8192], P(None, None, None, 'col'), may hold values from -0.5 to 0.5
- down_adapter_first: float32 [8, 16, 8192], P(None, None, 'col'), may hold values from -0.0625 to 0.0625
- down_adapter_second: float32 [8, 16, 2048], P(None, None, 'row'), may hold values from -0.5 to 0.5
Outputs:
- layer_out: bfloat16 [5120, 2048], P(('dp', 'col'), 'row')
- input_grad: float32 [5120, 2048], P(('dp', 'col'), 'row')
- grad_a_qkv: float32 [3, 8, 16, 2048], P(None, 'dp', 'col', 'row')
- grad_b_qkv: float32 [3, 8, 16, 2048], P(None, 'dp', 'row', 'col')
- grad_a_out: float32 [8, 16, 2048], P('dp', 'row', 'col')
- grad_b_out: float32 [8, 16, 2048], P('dp', 'col', 'row')
- grad_a_gu: float32 [2, 8, 16, 2048], P(None, 'dp', 'col', 'row')
- grad_b_gu: float32 [2, 8, 16, 8192], P(None, 'dp', 'row', 'col')
- grad_a_down: float32 [8, 16, 8192], P('dp', 'row', 'col')
- grad_b_down: float32 [8, 16, 2048], P('dp', 'col', 'row')
Inputs may be any that keep to these rules, and one draw needn't show every extreme that they name: `seg_ids`: in each tree the first 1024 tokens are segment 0, the trunk; the other 12 segments of 128 tokens each follow in any order: branches are 1 to 4, leaves the higher numbers. The trunk's tokens have positions 0 to 1023 in order, a branch's 1024 onward, a leaf's 1024 + 128 onward. `parents`: the trunk and the branches have parent 0; each leaf has a branch as parent, and each branch has 2 leaves.
All inputs are finite; a program needn't handle non-finite values.
Results may differ from a plain program's by a relative error of at most 0.025.
Values may be sent and summed in bfloat16 or wider, within the bound.
A program may use at most 320 MiB of HBM per device.

v0:
```python
import jax
import jax.numpy as jnp
from jax import lax
from jax.sharding import PartitionSpec as P

D = 2048
HEAD = 128
RANK = 16
epsilon = 1e-06
rope_base = 500000.0
masked_out = -1e30
low = jnp.bfloat16
wide = jnp.float32
last_last = (((1,), (1,)), ((), ()))
first_first = (((0,), (0,)), ((), ()))


def dot(left, right):
    return jnp.dot(left, right, preferred_element_type=wide)


def dot_t(left, right):
    return lax.dot_general(left, right, last_last, preferred_element_type=wide)


def t_dot(left, right):
    return lax.dot_general(left, right, first_first, preferred_element_type=wide)


def angles(positions):
    half_width = HEAD // 2
    frequency = rope_base ** (-(jnp.arange(half_width, dtype=wide) * 2.0) / HEAD)
    angle_table = positions.astype(wide)[:, None] * frequency[None, :]
    return (jnp.cos(angle_table)[:, None, :], jnp.sin(angle_table)[:, None, :])


def rotate(values, cosine, sine):
    half_width = values.shape[-1] // 2
    first_half = values[..., :half_width]
    second_half = values[..., half_width:]
    return jnp.concatenate(
        [first_half * cosine - second_half * sine, second_half * cosine + first_half * sine],
        axis=-1,
    )


def norm_factor(square_sum):
    return lax.rsqrt(square_sum / D + epsilon)


def norm_back(scaled, flat, factor, cross_sum):
    return factor[:, None] * (scaled - flat * (cross_sum / D)[:, None])


def tree_mask(seg_ids, positions, parents):
    parent_row = parents[0]
    labels = jnp.arange(parent_row.shape[0], dtype=jnp.int32)
    parent_tok = jnp.sum(
        jnp.where(seg_ids[:, None] == labels[None, :], parent_row[None, :], 0), axis=1
    )
    grand_tok = jnp.sum(
        jnp.where(parent_tok[:, None] == labels[None, :], parent_row[None, :], 0), axis=1
    )
    on_path = (
        (seg_ids[None, :] == seg_ids[:, None])
        | (seg_ids[None, :] == parent_tok[:, None])
        | (seg_ids[None, :] == grand_tok[:, None])
    )
    return on_path & (positions[None, :] <= positions[:, None])


def per_device(
    tokens,
    cotangent,
    seg_ids,
    positions,
    parents,
    tree_sets,
    gain_q,
    gain_k,
    gain_attn,
    gain_ffn,
    query_key_value_weight,
    output_weight,
    gate_up_weight,
    down_weight,
    query_key_value_adapter_first,
    query_key_value_adapter_second,
    output_adapter_first,
    output_adapter_second,
    gate_up_adapter_first,
    gate_up_adapter_second,
    down_adapter_first,
    down_adapter_second,
):
    dp_count = lax.axis_size("dp")
    row_count = lax.axis_size("row")
    col_count = lax.axis_size("col")
    row_at = lax.axis_index("row")
    tree_tokens = seg_ids.shape[0]
    assert tree_sets.shape[0] == 1
    set_count = output_adapter_first.shape[0]
    own = tokens.shape[0] // row_count
    group = own * col_count
    width_row = tokens.shape[1]
    width_col = gain_q.shape[0]
    hidden_col = down_weight.shape[0]
    heads_col = width_col // HEAD
    score_scale = HEAD ** (-0.5)
    tree_set = tree_sets[0]

    def pick(table, axis):
        return lax.dynamic_index_in_dim(table, tree_set, axis, keepdims=False)

    narrow = jnp.concatenate(
        [
            pick(query_key_value_adapter_first, 1),
            pick(gate_up_adapter_first, 1),
            pick(output_adapter_second, 0)[None],
            pick(down_adapter_second, 0)[None],
        ],
        axis=0,
    ).astype(low)
    narrow_all = lax.all_gather(narrow, "row", axis=2, tiled=True)
    a_qkv = narrow_all[:3].reshape(3 * RANK, D)
    a_gu = narrow_all[3:5].reshape(2 * RANK, D)
    b_out = narrow_all[5]
    b_down = narrow_all[6]
    b_qkv = pick(query_key_value_adapter_second, 1).astype(low)
    b_gu = pick(gate_up_adapter_second, 1).astype(low)
    a_out = pick(output_adapter_first, 0).astype(low)
    a_down = pick(down_adapter_first, 0).astype(low)
    gains = lax.all_gather(jnp.stack([gain_attn, gain_ffn]), "row", axis=1, tiled=True)
    w_qkv = lax.all_gather(query_key_value_weight, "row", axis=0, tiled=True).reshape(
        D, 3 * width_col
    )
    w_out = lax.all_gather(output_weight, "row", axis=1, tiled=True)
    w_gu = lax.all_gather(gate_up_weight, "row", axis=0, tiled=True).reshape(D, 2 * hidden_col)
    w_down = lax.all_gather(down_weight, "row", axis=1, tiled=True)

    def to_tokens(values):
        return lax.all_to_all(values, "row", split_axis=0, concat_axis=1, tiled=True)

    def to_width(values):
        return lax.all_to_all(values, "row", split_axis=1, concat_axis=0, tiled=True)

    def gather_col(values):
        return lax.all_gather(values, "col", axis=0, tiled=True)

    def scatter_col(values):
        return lax.psum_scatter(values.astype(low), "col", scatter_dimension=0, tiled=True).astype(
            wide
        )

    def to_heads(values, parts):
        by_head = (
            values.reshape(group, parts, heads_col, HEAD)
            .transpose(2, 0, 1, 3)
            .reshape(heads_col, group, parts * HEAD)
        )
        moved = lax.all_to_all(by_head, "row", split_axis=0, concat_axis=0, tiled=True)
        return (
            moved.reshape(row_count, col_count, own, parts * HEAD)
            .transpose(1, 0, 2, 3)
            .reshape(tree_tokens, parts * HEAD)
        )

    def from_heads(values, parts):
        by_row = (
            values.reshape(col_count, row_count, own, parts * HEAD)
            .transpose(1, 0, 2, 3)
            .reshape(row_count, group, parts * HEAD)
        )
        moved = lax.all_to_all(by_row, "row", split_axis=0, concat_axis=0, tiled=True)
        return (
            moved.reshape(heads_col, group, parts, HEAD)
            .transpose(1, 2, 0, 3)
            .reshape(group, parts * width_col)
        )

    x_own = to_tokens(tokens)
    x = gather_col(x_own)
    red_qkv = dot_t(x, a_qkv).astype(low)
    raw = dot(x, w_qkv)
    extra = jnp.concatenate(
        [dot(red_qkv[:, RANK * j : RANK * (j + 1)], b_qkv[j]) for j in range(3)], axis=1
    )
    raw = raw + extra
    q_raw = raw[:, :width_col]
    k_raw = raw[:, width_col : 2 * width_col]
    v_raw = raw[:, 2 * width_col :]
    square_qk = lax.psum(
        jnp.stack([jnp.sum(q_raw * q_raw, axis=1), jnp.sum(k_raw * k_raw, axis=1)]), "col"
    )
    q_factor = norm_factor(square_qk[0])
    k_factor = norm_factor(square_qk[1])
    q_flat = q_raw * q_factor[:, None]
    k_flat = k_raw * k_factor[:, None]
    pos_own = lax.dynamic_index_in_dim(
        positions.reshape(col_count, row_count, own), row_at, 1, keepdims=False
    ).reshape(group)
    cos_own, sin_own = angles(pos_own)

    def turn(values, sine):
        return rotate(values.reshape(group, heads_col, HEAD), cos_own, sine).reshape(
            group, width_col
        )

    q_low = turn(q_flat * gain_q, sin_own).astype(low)
    k_low = turn(k_flat * gain_k, sin_own).astype(low)
    qkv_head = to_heads(jnp.concatenate([q_low, k_low, v_raw.astype(low)], axis=1), 3)
    q_head = qkv_head[:, :HEAD]
    k_head = qkv_head[:, HEAD : 2 * HEAD]
    v_head = qkv_head[:, 2 * HEAD :]
    visible = tree_mask(seg_ids, positions, parents)
    scores = jnp.where(visible, dot_t(q_head, k_head) * score_scale, masked_out)
    highest = jnp.max(scores, axis=1, keepdims=True)
    raised = jnp.exp(scores - highest)
    probs = raised / jnp.sum(raised, axis=1, keepdims=True)
    probs_low = probs.astype(low)
    attn_head = dot(probs_low, v_head).astype(low)
    attn = from_heads(attn_head, 1)
    red_out = dot_t(attn, a_out).astype(low)
    a_raw = scatter_col(dot(attn, w_out) + dot(red_out, b_out))
    a_factor = norm_factor(jnp.sum(a_raw * a_raw, axis=1))
    a_flat = a_raw * a_factor[:, None]
    h_own = x_own.astype(wide) + a_flat * gains[0]
    h = gather_col(h_own.astype(low))
    red_gu = dot_t(h, a_gu).astype(low)
    gate = dot(h, w_gu[:, :hidden_col]) + dot(red_gu[:, :RANK], b_gu[0])
    up = dot(h, w_gu[:, hidden_col:]) + dot(red_gu[:, RANK:], b_gu[1])
    sigma = jax.nn.sigmoid(gate)
    hidden = (gate * sigma * up).astype(low)
    red_down = dot_t(hidden, a_down).astype(low)
    f_raw = scatter_col(dot(hidden, w_down) + dot(red_down, b_down))
    f_factor = norm_factor(jnp.sum(f_raw * f_raw, axis=1))
    f_flat = f_raw * f_factor[:, None]
    out_own = (h_own + f_flat * gains[1]).astype(low)
    layer_out = to_width(out_own)
    g_own = to_tokens(cotangent).astype(wide)
    scaled_f = g_own * gains[1]
    d_f_own = norm_back(scaled_f, f_flat, f_factor, jnp.sum(scaled_f * f_flat, axis=1)).astype(low)
    d_f = gather_col(d_f_own)
    back_down = dot_t(d_f, b_down).astype(low)
    d_hidden = dot_t(d_f, w_down) + dot(back_down, a_down)
    d_gate = (d_hidden * up * sigma * (1.0 + gate * (1.0 - sigma))).astype(low)
    d_up = (d_hidden * (gate * sigma)).astype(low)
    back_gate = dot_t(d_gate, b_gu[0]).astype(low)
    back_up = dot_t(d_up, b_gu[1]).astype(low)
    back_gu = jnp.concatenate([back_gate, back_up], axis=1)
    d_h = g_own + scatter_col(
        dot_t(d_gate, w_gu[:, :hidden_col]) + dot_t(d_up, w_gu[:, hidden_col:]) + dot(back_gu, a_gu)
    )
    scaled_a = d_h * gains[0]
    d_a_own = norm_back(scaled_a, a_flat, a_factor, jnp.sum(scaled_a * a_flat, axis=1)).astype(low)
    d_a = gather_col(d_a_own)
    back_out = dot_t(d_a, b_out).astype(low)
    d_attn = (dot_t(d_a, w_out) + dot(back_out, a_out)).astype(low)
    d_attn_head = to_heads(d_attn, 1)
    d_probs = dot_t(d_attn_head, v_head)
    inner = jnp.sum(probs * d_probs, axis=1, keepdims=True)
    d_scores = (probs * (d_probs - inner)).astype(low)
    dq_head = (dot(d_scores, k_head) * score_scale).astype(low)
    dk_head = (t_dot(d_scores, q_head) * score_scale).astype(low)
    dv_head = t_dot(probs_low, d_attn_head).astype(low)
    d_qkv = from_heads(jnp.concatenate([dq_head, dk_head, dv_head], axis=1), 3)
    dq_n = turn(d_qkv[:, :width_col].astype(wide), -sin_own) * gain_q
    dk_n = turn(d_qkv[:, width_col : 2 * width_col].astype(wide), -sin_own) * gain_k
    cross_qk = lax.psum(
        jnp.stack([jnp.sum(dq_n * q_flat, axis=1), jnp.sum(dk_n * k_flat, axis=1)]), "col"
    )
    d_q = norm_back(dq_n, q_flat, q_factor, cross_qk[0]).astype(low)
    d_k = norm_back(dk_n, k_flat, k_factor, cross_qk[1]).astype(low)
    d_v = d_qkv[:, 2 * width_col :]
    d_raw = jnp.concatenate([d_q, d_k, d_v], axis=1)
    back_qkv = jnp.concatenate(
        [dot_t(d, b) for d, b in zip((d_q, d_k, d_v), (b_qkv[0], b_qkv[1], b_qkv[2]))], axis=1
    ).astype(low)
    in_own = d_h + scatter_col(dot_t(d_raw, w_qkv) + dot(back_qkv, a_qkv))
    input_grad = to_width(in_own.astype(low)).astype(wide)
    full_width = jnp.concatenate(
        [t_dot(back_qkv, x), t_dot(back_gu, h), t_dot(red_out, d_a), t_dot(red_down, d_f)], axis=0
    ).astype(low)
    full_width = lax.psum_scatter(full_width, "row", scatter_dimension=1, tiled=True)
    full_width = full_width.reshape(7, col_count, RANK // col_count, width_row).transpose(
        1, 0, 2, 3
    )
    full_width = lax.psum_scatter(full_width, "col", scatter_dimension=0, tiled=False)
    col_width = jnp.concatenate(
        [t_dot(red_qkv[:, RANK * j : RANK * (j + 1)], d) for j, d in enumerate((d_q, d_k, d_v))]
        + [
            t_dot(back_out, attn),
            t_dot(red_gu[:, :RANK], d_gate),
            t_dot(red_gu[:, RANK:], d_up),
            t_dot(back_down, hidden),
        ],
        axis=1,
    ).astype(low)
    col_width = lax.psum_scatter(col_width, "row", scatter_dimension=0, tiled=True)
    onehot = (tree_set == jnp.arange(set_count, dtype=jnp.int32)).astype(wide)
    owner = jnp.concatenate([full_width.reshape(-1), col_width.reshape(-1)])
    owner_all = lax.all_gather(owner, "dp", axis=0, tiled=False).astype(wide)
    onehot_all = lax.all_gather(onehot, "dp", axis=0, tiled=False)
    sets_own = set_count // dp_count
    onehot_own = lax.dynamic_slice_in_dim(onehot_all, lax.axis_index("dp") * sets_own, sets_own, 1)
    per_set = jnp.sum(onehot_own[:, :, None] * owner_all[:, None, :], axis=0)
    split_at = full_width.size
    full_sets = per_set[:, :split_at].reshape(sets_own, 7, RANK // col_count, width_row)
    col_sets = per_set[:, split_at:].reshape(sets_own, RANK // row_count, -1)
    grad_a_qkv = full_sets[:, :3].transpose(1, 0, 2, 3)
    grad_a_gu = full_sets[:, 3:5].transpose(1, 0, 2, 3)
    grad_b_out = full_sets[:, 5]
    grad_b_down = full_sets[:, 6]
    grad_b_qkv = jnp.stack([col_sets[..., width_col * j : width_col * (j + 1)] for j in range(3)])
    grad_a_out = col_sets[..., 3 * width_col : 4 * width_col]
    gu_at = 4 * width_col
    grad_b_gu = jnp.stack(
        [col_sets[..., gu_at + hidden_col * j : gu_at + hidden_col * (j + 1)] for j in range(2)]
    )
    grad_a_down = col_sets[..., gu_at + 2 * hidden_col :]
    return (
        layer_out,
        input_grad,
        grad_a_qkv,
        grad_b_qkv,
        grad_a_out,
        grad_b_out,
        grad_a_gu,
        grad_b_gu,
        grad_a_down,
        grad_b_down,
    )


def solution(mesh):
    in_specs = (
        P(("dp", "col"), "row"),
        P(("dp", "col"), "row"),
        P("dp"),
        P("dp"),
        P("dp", None),
        P("dp"),
        P("col"),
        P("col"),
        P("row"),
        P("row"),
        P("row", None, "col"),
        P("col", "row"),
        P("row", None, "col"),
        P("col", "row"),
        P(None, None, None, "row"),
        P(None, None, None, "col"),
        P(None, None, "col"),
        P(None, None, "row"),
        P(None, None, None, "row"),
        P(None, None, None, "col"),
        P(None, None, "col"),
        P(None, None, "row"),
    )
    out_specs = (
        P(("dp", "col"), "row"),
        P(("dp", "col"), "row"),
        P(None, "dp", "col", "row"),
        P(None, "dp", "row", "col"),
        P("dp", "row", "col"),
        P("dp", "col", "row"),
        P(None, "dp", "col", "row"),
        P(None, "dp", "row", "col"),
        P("dp", "row", "col"),
        P("dp", "col", "row"),
    )
    return jax.shard_map(
        per_device, mesh=mesh, in_specs=in_specs, out_specs=out_specs, check_vma=False
    )
```

profile of v0, /device:TPU:0, one launch (start us, length us, event | category | flops | bytes accessed | tf_op | source)
XLA Modules:
  0.0 1157.8 jit_solution(14469267757178420043)
XLA Ops:
  7.2 14.6 %all_to_all.84 = bf16[4,160,512]{2,1,0:T(8,128)(2,1)S(1)} all-to-all(bf16[4,160,512]{2,1,0:T(8,128)(2,1)} %bitcast.270), channel_id=1, replica_groups=mesh['dp'=2,'row'=4,'col'=4] {'row'}, dimensions={0} | all-to-all | bytes 1310720 | tf_op jit(solution)/shard_map/all_to_all | solution.py:142
  39.2 39.6 %all-gather.11.cloned.1.call-done = bf16[640,2048]{1,0:T(8,128)(2,1)} async-done(((bf16[160,2048]{1,0:T(8,128)(2,1)}), bf16[640,2048]{1,0:T(8,128)(2,1)}) %all-gather.11.cloned.1.call-update) | async-done | bytes 2621456 | tf_op jit(solution)/shard_map/all_gather | solution.py:148
  84.6 40.9 %all-gather.13.cloned.1.call-done = bf16[2048,3,512]{0,2,1:T(8,128)(2,1)} async-done(((bf16[512,3,512]{0,2,1:T(8,128)(2,1)}), bf16[2048,3,512]{0,2,1:T(8,128)(2,1)}) %all-gather.13.cloned.1.call-update) | async-done | bytes 6291472 | tf_op jit(solution)/shard_map/all_gather | solution.py:134
  137.0 12.3 %psum.14 = f32[2,640]{1,0:T(2,128)S(1)} all-reduce(f32[2,640]{1,0:T(2,128)S(1)} %pad_maximum_fusion.17), channel_id=1, replica_groups=mesh['dp'=2,'row'=4,'col'=4] {'col'}, use_global_device_ids=true, to_apply=%region_4.5 | all-reduce | flops 1280 | bytes 10240 | tf_op jit(solution)/shard_map/psum | solution.py:192
  179.6 34.4 %all-to-all-done.1 = bf16[4,640,384]{1,2,0:T(8,128)(2,1)} async-done(((bf16[4,640,384]{1,2,0:T(8,128)(2,1)}), bf16[4,640,384]{1,2,0:T(8,128)(2,1)}, u32[]{:S(2)}, u32[]{:S(2)}) %all-to-all-start.1) | async-done | bytes 1966112 | tf_op jit(solution)/shard_map/all_to_all | solution.py:161
  251.8 12.7 %all_to_all.85 = bf16[4,640,128]{2,1,0:T(8,128)(2,1)S(1)} all-to-all(bf16[4,640,128]{2,1,0:T(8,128)(2,1)S(1)} %bitcast.254), channel_id=1, replica_groups=mesh['dp'=2,'row'=4,'col'=4] {'row'}, dimensions={0} | all-to-all | bytes 1310720 | tf_op jit(solution)/shard_map/all_to_all | solution.py:174
  278.0 43.6 %reduce-scatter.7.cloned.1.call-done = bf16[160,2048]{1,0:T(8,128)(2,1)} async-done(((bf16[640,2048]{1,0:T(8,128)(2,1)}), bf16[160,2048]{1,0:T(8,128)(2,1)}) %reduce-scatter.7.cloned.1.call-update) | async-done | bytes 655376 | tf_op jit(solution)/shard_map/reduce_scatter | solution.py:151
  327.8 52.1 %all-gather.17.cloned.1.call-done = bf16[640,2048]{1,0:T(8,128)(2,1)} async-done(((bf16[160,2048]{1,0:T(8,128)(2,1)}), bf16[640,2048]{1,0:T(8,128)(2,1)}) %all-gather.17.cloned.1.call-update) | async-done | bytes 2621456 | tf_op jit(solution)/shard_map/all_gather | solution.py:148
  382.5 103.5 %all-gather.19.cloned.1.call-done = bf16[2048,2,2048]{2,1,0:T(2,128)(2,1)} async-done(((bf16[512,2,2048]{2,1,0:T(2,128)(2,1)}), bf16[2048,2,2048]{2,1,0:T(2,128)(2,1)}) %all-gather.19.cloned.1.call-update) | async-done | bytes 16777232 | tf_op jit(solution)/shard_map/all_gather | solution.py:138
  486.0 13.0 %copy.133 = bf16[256,8,2,2048]{3,1,2,0:T(8,128)(2,1)S(1)} copy(bf16[256,8,2,2048]{3,2,1,0:T(2,128)(2,1)} %bitcast.231) | data formatting | bytes 33554432
  525.4 20.5 %all-gather.21.cloned.1.call-done = bf16[2048,2048]{1,0:T(8,128)(2,1)} async-done(((bf16[2048,512]{1,0:T(8,128)(2,1)}), bf16[2048,2048]{1,0:T(8,128)(2,1)}) %all-gather.21.cloned.1.call-update) | async-done | bytes 8388624 | tf_op jit(solution)/shard_map/all_gather | solution.py:139
  559.0 12.6 %all_to_all.86 = bf16[4,160,512]{2,1,0:T(8,128)(2,1)S(1)} all-to-all(bf16[4,160,512]{2,1,0:T(8,128)(2,1)S(1)} %bitcast.271), channel_id=1, replica_groups=mesh['dp'=2,'row'=4,'col'=4] {'row'}, dimensions={0} | all-to-all | bytes 1310720 | tf_op jit(solution)/shard_map/all_to_all | solution.py:142
  571.9 38.2 %reduce-scatter.9.cloned.1.call-done = bf16[160,2048]{1,0:T(8,128)(2,1)} async-done(((bf16[640,2048]{1,0:T(8,128)(2,1)}), bf16[160,2048]{1,0:T(8,128)(2,1)}) %reduce-scatter.9.cloned.1.call-update) | async-done | bytes 655376 | tf_op jit(solution)/shard_map/reduce_scatter | solution.py:151
  614.8 54.1 %all-gather.23.cloned.1.call-done = bf16[640,2048]{1,0:T(8,128)(2,1)} async-done(((bf16[160,2048]{1,0:T(8,128)(2,1)}), bf16[640,2048]{1,0:T(8,128)(2,1)}) %all-gather.23.cloned.1.call-update) | async-done | bytes 2621456 | tf_op jit(solution)/shard_map/all_gather | solution.py:148
  716.6 51.0 %reduce-scatter.11.cloned.1.call-done = bf16[160,2048]{1,0:T(8,128)(2,1)} async-done(((bf16[640,2048]{1,0:T(8,128)(2,1)}), bf16[160,2048]{1,0:T(8,128)(2,1)}) %reduce-scatter.11.cloned.1.call-update) | async-done | bytes 655376 | tf_op jit(solution)/shard_map/reduce_scatter | solution.py:151
  772.2 54.6 %all-gather.25.cloned.1.call-done = bf16[640,2048]{1,0:T(8,128)(2,1)} async-done(((bf16[160,2048]{1,0:T(8,128)(2,1)}), bf16[640,2048]{1,0:T(8,128)(2,1)}) %all-gather.25.cloned.1.call-update) | async-done | bytes 2621456 | tf_op jit(solution)/shard_map/all_gather | solution.py:148
  834.3 12.8 %all_to_all.87 = bf16[4,640,128]{2,1,0:T(8,128)(2,1)S(1)} all-to-all(bf16[4,640,128]{2,1,0:T(8,128)(2,1)S(1)} %bitcast.256), channel_id=1, replica_groups=mesh['dp'=2,'row'=4,'col'=4] {'row'}, dimensions={0} | all-to-all | bytes 1310720 | tf_op jit(solution)/shard_map/all_to_all | solution.py:161
  847.2 11.3 fusion.20
  858.5 20.5 %multiply_reduce_fusion = (f32[2560]{0:T(1024)S(1)}, f32[2560,2560]{0,1:T(8,128)}) fusion(f32[2560]{0:T(1024)S(1)} %copy-done.64, f32[2560,2560]{0,1:T(8,128)} %copy-done.2, f32[2560]{0:T(1024)S(1)} %copy-done.62, bf16[2560,128]{1,0:T(8,128)(2,1)S(1)} %bitcast.273, bf16[2560,384]{1,0:T(8,128)(2,1)S(1)} %bitcast.249), kind=kOutput, calls=%fused_computation.1 | convolution fusion | flops 1703933440 | bytes 53774336 | tf_op jit(solution)/shard_map/dot_general | solution.py:23
  878.9 22.4 %multiply_convert_fusion = bf16[2560,2560]{0,1:T(8,128)(2,1)} fusion(f32[2560,2560]{0,1:T(8,128)} %get-tuple-element.100, f32[2560]{0:T(1024)S(1)} %get-tuple-element.99, f32[2560]{0:T(1024)S(1)} %copy-done.64, f32[2560,2560]{0,1:T(8,128)} %copy-done.2, f32[2560]{0:T(1024)S(1)} %copy-done.62), kind=kLoop, calls=%fused_computation | loop fusion | flops 32768000 | bytes 65566720 | tf_op jit(solution)/shard_map/convert_element_type | solution.py:262
  933.0 17.8 %all-to-all-done.6 = bf16[4,640,384]{2,1,0:T(8,128)(2,1)S(1)} async-done(((bf16[4,640,384]{2,1,0:T(8,128)(2,1)}), bf16[4,640,384]{2,1,0:T(8,128)(2,1)S(1)}, u32[]{:S(2)}, u32[]{:S(2)}) %all-to-all-start.6) | async-done | bytes 1966112 | tf_op jit(solution)/shard_map/all_to_all | solution.py:174
  1028.9 12.6 %all-reduce.7.cloned.1.call-done = bf16[16,8192]{1,0:T(8,128)(2,1)} async-done(((bf16[16,8192]{1,0:T(8,128)(2,1)}), bf16[16,8192]{1,0:T(8,128)(2,1)}) %all-reduce.7.cloned.1.call-update) | async-done | bytes 262160
  1042.4 36.0 %all-reduce.5.cloned.1.call-done = bf16[4,7,4,512]{3,2,0,1:T(4,128)(2,1)} async-done(((bf16[4,7,4,512]{3,2,0,1:T(4,128)(2,1)}), bf16[4,7,4,512]{3,2,0,1:T(4,128)(2,1)}) %all-reduce.5.cloned.1.call-update) | async-done | bytes 114704
  1091.2 41.5 %reduce-scatter.13.cloned.1.call-done = bf16[160,2048]{1,0:T(8,128)(2,1)} async-done(((bf16[640,2048]{1,0:T(8,128)(2,1)}), bf16[160,2048]{1,0:T(8,128)(2,1)}) %reduce-scatter.13.cloned.1.call-update) | async-done | bytes 655376 | tf_op jit(solution)/shard_map/reduce_scatter | solution.py:151
  (356 shorter events, 368.4 us)
Async XLA Ops:
  7.2 320.6 %copy-start = (f32[2,8,16,2048]{3,2,1,0:T(8,128)S(1)}, f32[2,8,16,2048]{3,2,1,0:T(8,128)}, u32[]{:S(2)}) copy-start(f32[2,8,16,2048]{3,2,1,0:T(8,128)} %param.41) | copy-start | bytes 6291460
  7.2 71.5 %all-gather.11.cloned.1.call-start = ((), (), s32[]{:S(2)}) async-start(), calls=%async_computation.13 | async-start | bytes 3276800 | tf_op jit(solution)/shard_map/all_gather | solution.py:148
  22.8 102.7 %all-gather.13.cloned.1.call-start = ((), (), s32[]{:S(2)}) async-start(), calls=%async_computation.14 | async-start | bytes 7864320 | tf_op jit(solution)/shard_map/all_gather | solution.py:134
  173.8 40.1 %all-to-all-start.1 = ((bf16[4,640,384]{1,2,0:T(8,128)(2,1)}), bf16[4,640,384]{1,2,0:T(8,128)(2,1)}, u32[]{:S(2)}, u32[]{:S(2)}) async-start(bf16[4,640,384]{1,2,0:T(8,128)(2,1)} %bitcast.242), calls=%async_computation.1 | async-start | bytes 3932160 | tf_op jit(solution)/shard_map/all_to_all | solution.py:161
  178.4 87.4 %all-gather.15.cloned.1.call-start = ((), (), s32[]{:S(2)}) async-start(), calls=%async_computation.15 | async-start | bytes 2621440 | tf_op jit(solution)/shard_map/all_gather | solution.py:137
  179.1 142.5 %reduce-scatter.7.cloned.1.call-start = ((), (), s32[]{:S(2)}) async-start(), calls=%async_computation.16 | async-start | bytes 3276800 | tf_op jit(solution)/shard_map/reduce_scatter | solution.py:151
  272.1 50.8 %copy-start.20 = (bf16[4,20,8,512]{3,2,0,1:T(8,128)(2,1)S(1)}, bf16[4,20,8,512]{3,2,0,1:T(8,128)(2,1)}, u32[]{:S(2)}) copy-start(bf16[4,20,8,512]{3,2,0,1:T(8,128)(2,1)} %copy.129) | copy-start | bytes 1966084
  272.1 107.7 %all-gather.17.cloned.1.call-start = ((), (), s32[]{:S(2)}) async-start(), calls=%async_computation.17 | async-start | bytes 3276800 | tf_op jit(solution)/shard_map/all_gather | solution.py:148
  325.2 160.8 %all-gather.19.cloned.1.call-start = ((), (), s32[]{:S(2)}) async-start(), calls=%async_computation.18 | async-start | bytes 20971520 | tf_op jit(solution)/shard_map/all_gather | solution.py:138
  325.8 220.1 %all-gather.21.cloned.1.call-start = ((), (), s32[]{:S(2)}) async-start(), calls=%async_computation.19 | async-start | bytes 10485760 | tf_op jit(solution)/shard_map/all_gather | solution.py:139
  326.6 283.6 %reduce-scatter.9.cloned.1.call-start = ((), (), s32[]{:S(2)}) async-start(), calls=%async_computation.20 | async-start | bytes 3276800 | tf_op jit(solution)/shard_map/reduce_scatter | solution.py:151
  382.5 134.7 %copy-start.48 = (bf16[640,32]{0,1:T(8,128)(2,1)}, bf16[640,32]{0,1:T(8,128)(2,1)S(1)}, u32[]{:S(2)}) copy-start(bf16[640,32]{0,1:T(8,128)(2,1)S(1)} %convolution_convert_fusion.8) | copy-start | bytes 122884
  557.9 111.0 %all-gather.23.cloned.1.call-start = ((), (), s32[]{:S(2)}) async-start(), calls=%async_computation.21 | async-start | bytes 3276800 | tf_op jit(solution)/shard_map/all_gather | solution.py:148
  571.9 197.2 %copy-start.3 = (f32[4,20,8,512]{3,2,0,1:T(8,128)}, f32[4,20,8,512]{3,2,0,1:T(8,128)S(1)}, u32[]{:S(2)}) copy-start(f32[4,20,8,512]{3,2,0,1:T(8,128)S(1)} %copy.130) | copy-start | bytes 3932164
  614.3 153.3 %reduce-scatter.11.cloned.1.call-start = ((), (), s32[]{:S(2)}) async-start(), calls=%async_computation.22 | async-start | bytes 3276800 | tf_op jit(solution)/shard_map/reduce_scatter | solution.py:151
  716.5 51.1 %copy-start.21 = (bf16[160,2048]{1,0:T(8,128)(2,1)S(1)}, bf16[160,2048]{1,0:T(8,128)(2,1)}, u32[]{:S(2)}) copy-start(bf16[160,2048]{1,0:T(8,128)(2,1)} %reduce-scatter.7.cloned.1.call-done) | copy-start | bytes 1966084
  716.5 110.3 %all-gather.25.cloned.1.call-start = ((), (), s32[]{:S(2)}) async-start(), calls=%async_computation.23 | async-start | bytes 3276800 | tf_op jit(solution)/shard_map/all_gather | solution.py:148
  922.8 28.0 %all-to-all-start.6 = ((bf16[4,640,384]{2,1,0:T(8,128)(2,1)}), bf16[4,640,384]{2,1,0:T(8,128)(2,1)S(1)}, u32[]{:S(2)}, u32[]{:S(2)}) async-start(bf16[4,640,384]{2,1,0:T(8,128)(2,1)} %bitcast.243), calls=%async_computation.9 | async-start | bytes 3932160 | tf_op jit(solution)/shard_map/all_to_all | solution.py:174
  926.6 79.7 %reduce-scatter.15.cloned.1.call-start = ((), (), s32[]{:S(2)}) async-start(), calls=%async_computation.25 | async-start | bytes 573440 | tf_op jit(solution)/shard_map/reduce_scatter | solution.py:284
  987.2 54.2 %all-reduce.7.cloned.1.call-start = ((), (), s32[]{:S(2)}) async-start(), calls=%async_computation.27 | async-start | bytes 524288
  993.5 84.9 %all-reduce.5.cloned.1.call-start = ((), (), s32[]{:S(2)}) async-start(), calls=%async_computation.26 | async-start | bytes 229376
  1007.8 124.9 %reduce-scatter.13.cloned.1.call-start = ((), (), s32[]{:S(2)}) async-start(), calls=%async_computation.24 | async-start | bytes 3276800 | tf_op jit(solution)/shard_map/reduce_scatter | solution.py:151
  1014.8 14.1 %all-to-all-start.3 = ((bf16[160,4,512]{2,0,1:T(8,128)(2,1)}), bf16[160,4,512]{2,0,1:T(8,128)(2,1)S(1)}, u32[]{:S(2)}, u32[]{:S(2)}) async-start(bf16[160,4,512]{2,0,1:T(8,128)(2,1)} %bitcast.215), calls=%async_computation.5 | async-start | bytes 1310720 | tf_op jit(solution)/shard_map/all_to_all | solution.py:145
  1135.0 13.8 %all-to-all-start.7 = ((bf16[160,4,512]{2,0,1:T(8,128)(2,1)}), bf16[160,4,512]{2,0,1:T(8,128)(2,1)S(1)}, u32[]{:S(2)}, u32[]{:S(2)}) async-start(bf16[160,4,512]{2,0,1:T(8,128)(2,1)} %bitcast.214), calls=%async_computation.11 | async-start | bytes 1310720 | tf_op jit(solution)/shard_map/all_to_all | solution.py:145
  (75 other events, 678.3 us)
Sparse Core Ops, SparseCore 0:
  22.9 55.7 all-gather.10
  80.3 45.1 all-gather.12
  180.8 32.5 all-gather.14
  272.3 49.3 reduce-scatter.6
  325.3 54.4 all-gather.16
  381.3 104.6 all-gather.18
  487.6 58.2 all-gather.20
  558.1 52.0 reduce-scatter.8
  614.4 54.4 all-gather.22
  716.7 50.8 reduce-scatter.10
  772.3 54.4 all-gather.24
  987.4 18.8 reduce-scatter.14
  1009.1 32.2 all-reduce.6
  1044.3 34.0 all-reduce.4
  1080.6 52.0 reduce-scatter.12
where the time goes:
time: 1170 us; the launch traced here: 1160 us
  waiting for transfers between devices  654 us (56%)
  matrix products  212 us (18%)
  local copies, waits for them, and re-layouts  96.2 us (8%)
  blocking collectives  95.6 us (8%)
  other arithmetic  66.5 us (6%)
  starting transfers between devices  16.8 us (1%)
  between operations  16.8 us (1%)
    all_gather x4, waiting for transfers between devices, gather_col(): return lax.all_gather(values, 'col', axis=0, tiled=True)  200 us
    reduce_scatter x4, waiting for transfers between devices, scatter_col(): lax.psum_scatter(values.astype(low), 'col', scatter_dimension=0, tiled=True)  174 us
    all_gather x1, waiting for transfers between devices, per_device(): lax.all_gather(gate_up_weight, 'row', axis=0, tiled=True)  104 us
    dot_general x18, matrix products, dot(): return jnp.dot(left, right, preferred_element_type=wide)  93.1 us
    dot_general x18, matrix products, dot_t(): return lax.dot_general(left, right, last_last, preferred_element_type=wide)  84.5 us
    unnamed x17, waiting for transfers between devices  50.7 us
    unnamed x173, local copies, waits for them, and re-layouts  41 us
    all_gather x1, waiting for transfers between devices, per_device(): lax.all_gather(query_key_value_weight, 'row', axis=0, tiled=True)  40.9 us
  transfers between devices with their start and end apart: 19, of which 18 were waited for; matrix products, arithmetic and copies ran while one was open for 11% of the time, Pallas kernels for 0%

commit v1 on v0

--- a/solution.py
+++ b/solution.py
@@ -13,6 +13,18 @@
 wide = jnp.float32
 last_last = (((1,), (1,)), ((), ()))
 first_first = (((0,), (0,)), ((), ()))
+
+
+def doubled_up(x, axis, dim):
+    ways, here = (lax.axis_size(axis), lax.axis_index(axis))
+    grown, reach = (x, 1)
+    while reach < ways:
+        theirs = lax.ppermute(grown, axis, [(d, d ^ reach) for d in range(ways)])
+        mine_first = jnp.concatenate([grown, theirs], axis=dim)
+        theirs_first = jnp.concatenate([theirs, grown], axis=dim)
+        grown = jnp.where(here & reach == 0, mine_first, theirs_first)
+        reach = 2 * reach
+    return grown
 
 
 def dot(left, right):
@@ -135,7 +147,7 @@
         D, 3 * width_col
     )
     w_out = lax.all_gather(output_weight, "row", axis=1, tiled=True)
-    w_gu = lax.all_gather(gate_up_weight, "row", axis=0, tiled=True).reshape(D, 2 * hidden_col)
+    w_gu = doubled_up(gate_up_weight, "row", 0).reshape(D, 2 * hidden_col)
     w_down = lax.all_gather(down_weight, "row", axis=1, tiled=True)
 
     def to_tokens(values):

time: 1170 us -> 1260 us (1.077)
  other arithmetic: 66.5 us -> 112 us
  waiting for transfers between devices: 654 us -> 672 us
  starting transfers between devices: 16.8 us -> 29.5 us
    ppermute x0 -> x2, waiting for transfers between devices: none -> 198 us  [doubled_up(): theirs = lax.ppermute(grown, axis, [(d, d ^ reach) for d in range(ways)])]
    all_gather x1 -> x0, waiting for transfers between devices: 104 us -> none  [per_device(): lax.all_gather(gate_up_weight, 'row', axis=0, tiled=True)]
    all_gather x4, waiting for transfers between devices: 200 us -> 149 us  [gather_col(): return lax.all_gather(values, 'col', axis=0, tiled=True)]
    select_n x0 -> x3, other arithmetic: none -> 46.2 us  [doubled_up(): grown = jnp.where(here & reach == 0, mine_first, theirs_first)]
    all_gather x1, waiting for transfers between devices: 20.5 us -> 0.01 us  [per_device(): w_down = lax.all_gather(down_weight, 'row', axis=1, tiled=True)]
    unnamed x173 -> x179, local copies, waits for them, and re-layouts: 41 us -> 49.8 us
    unnamed x17 -> x16, waiting for transfers between devices: 50.7 us -> 49.4 us
  transfers between devices with their start and end apart: 19 -> 20, of which waited for: 18 -> 16; matrix products, arithmetic and copies ran while one was open for 11% -> 16% of each run, Pallas kernels for 0% -> 0%
where the time goes in v1:
time: 1260 us; the launch traced here: 1250 us
  waiting for transfers between devices  672 us (53%)
  matrix products  217 us (17%)
  other arithmetic  112 us (9%)
  local copies, waits for them, and re-layouts  105 us (8%)
  blocking collectives  97.9 us (8%)
  starting transfers between devices  29.5 us (2%)
  between operations  16.9 us (1%)
    ppermute x2, waiting for transfers between devices, doubled_up(): theirs = lax.ppermute(grown, axis, [(d, d ^ reach) for d in range(ways)])  198 us
    reduce_scatter x4, waiting for transfers between devices, scatter_col(): lax.psum_scatter(values.astype(low), 'col', scatter_dimension=0, tiled=True)  172 us
    all_gather x4, waiting for transfers between devices, gather_col(): return lax.all_gather(values, 'col', axis=0, tiled=True)  149 us
    dot_general x18, matrix products, dot(): return jnp.dot(left, right, preferred_element_type=wide)  94 us
    dot_general x18, matrix products, dot_t(): return lax.dot_general(left, right, last_last, preferred_element_type=wide)  88.6 us
    unnamed x179, local copies, waits for them, and re-layouts  49.8 us
    unnamed x16, waiting for transfers between devices  49.4 us
    select_n x3, other arithmetic, doubled_up(): grown = jnp.where(here & reach == 0, mine_first, theirs_first)  46.2 us
  transfers between devices with their start and end apart: 20, of which 16 were waited for; matrix products, arithmetic and copies ran while one was open for 16% of the time, Pallas kernels for 0%

profile of v1, /device:TPU:0, one launch (start us, length us, event | category | flops | bytes accessed | tf_op | source)
XLA Modules:
  0.0 1250.8 jit_solution(6102220294882803389)
XLA Ops:
  7.2 14.6 %all_to_all.84 = bf16[4,160,512]{2,1,0:T(8,128)(2,1)S(1)} all-to-all(bf16[4,160,512]{2,1,0:T(8,128)(2,1)} %bitcast.273), channel_id=1, replica_groups=mesh['dp'=2,'row'=4,'col'=4] {'row'}, dimensions={0} | all-to-all | bytes 1310720 | tf_op jit(solution)/shard_map/all_to_all | solution.py:154
  39.2 39.5 %all-gather.10.cloned.1.call-done = bf16[640,2048]{1,0:T(8,128)(2,1)} async-done(((bf16[160,2048]{1,0:T(8,128)(2,1)}), bf16[640,2048]{1,0:T(8,128)(2,1)}) %all-gather.10.cloned.1.call-update) | async-done | bytes 2621456 | tf_op jit(solution)/shard_map/all_gather | solution.py:160
  84.6 40.9 %all-gather.12.cloned.1.call-done = bf16[2048,3,512]{0,2,1:T(8,128)(2,1)} async-done(((bf16[512,3,512]{0,2,1:T(8,128)(2,1)}), bf16[2048,3,512]{0,2,1:T(8,128)(2,1)}) %all-gather.12.cloned.1.call-update) | async-done | bytes 6291472 | tf_op jit(solution)/shard_map/all_gather | solution.py:146
  136.8 12.0 psum.14
  178.9 34.2 %all-to-all-done.1 = bf16[4,640,384]{1,2,0:T(8,128)(2,1)} async-done(((bf16[4,640,384]{1,2,0:T(8,128)(2,1)}), bf16[4,640,384]{1,2,0:T(8,128)(2,1)}, u32[]{:S(2)}, u32[]{:S(2)}) %all-to-all-start.1) | async-done | bytes 1966112 | tf_op jit(solution)/shard_map/all_to_all | solution.py:173
  251.0 12.7 %all_to_all.85 = bf16[4,640,128]{2,1,0:T(8,128)(2,1)S(1)} all-to-all(bf16[4,640,128]{2,1,0:T(8,128)(2,1)S(1)} %bitcast.257), channel_id=1, replica_groups=mesh['dp'=2,'row'=4,'col'=4] {'row'}, dimensions={0} | all-to-all | bytes 1310720 | tf_op jit(solution)/shard_map/all_to_all | solution.py:186
  279.5 41.4 %reduce-scatter.7.cloned.1.call-done = bf16[160,2048]{1,0:T(8,128)(2,1)} async-done(((bf16[640,2048]{1,0:T(8,128)(2,1)}), bf16[160,2048]{1,0:T(8,128)(2,1)}) %reduce-scatter.7.cloned.1.call-update) | async-done | bytes 655376 | tf_op jit(solution)/shard_map/reduce_scatter | solution.py:163
  324.6 21.1 %broadcast_select_fusion = bf16[1024,2,2048]{2,1,0:T(2,128)(2,1)} fusion(pred[]{:T(512)S(6)} %eq.94, bf16[512,2,2048]{2,1,0:T(2,128)(2,1)} %collective-permute-done, bf16[512,2,2048]{2,1,0:T(2,128)(2,1)} %param.34), kind=kLoop, calls=%fused_computation.7 | loop fusion | flops 12582912 | bytes 16777216 | tf_op jit(solution)/shard_map/jit(_where)/select_n | solution.py:25
  375.3 197.7 %collective-permute-done.1 = bf16[1024,2,2048]{2,1,0:T(2,128)(2,1)} collective-permute-done((bf16[1024,2,2048]{2,1,0:T(2,128)(2,1)}, bf16[1024,2,2048]{2,1,0:T(2,128)(2,1)}, u32[]{:S(2)}, u32[]{:S(2)}) %collective-permute-start.1) | collective-permute-done | bytes 8388640 | tf_op jit(solution)/shard_map/ppermute | solution.py:22
  573.0 12.0 copy.135
  585.1 18.8 %maximum_select_fusion = bf16[2048,4096]{1,0:T(8,128)(2,1)} fusion(bf16[1024,4096]{1,0:T(8,128)(2,1)} %bitcast.227, bf16[1024,4096]{1,0:T(8,128)(2,1)} %maximum_select_fusion.1, pred[]{:T(512)S(6)} %eq.93), kind=kLoop, calls=%fused_computation.6 | loop fusion | flops 75497472 | bytes 33554432 | tf_op jit(solution)/shard_map/jit(_where)/select_n | solution.py:25
  652.3 12.8 %all_to_all.86 = bf16[4,160,512]{2,1,0:T(8,128)(2,1)S(1)} all-to-all(bf16[4,160,512]{2,1,0:T(8,128)(2,1)S(1)} %bitcast.274), channel_id=1, replica_groups=mesh['dp'=2,'row'=4,'col'=4] {'row'}, dimensions={0} | all-to-all | bytes 1310720 | tf_op jit(solution)/shard_map/all_to_all | solution.py:154
  665.3 38.0 %reduce-scatter.9.cloned.1.call-done = bf16[160,2048]{1,0:T(8,128)(2,1)} async-done(((bf16[640,2048]{1,0:T(8,128)(2,1)}), bf16[160,2048]{1,0:T(8,128)(2,1)}) %reduce-scatter.9.cloned.1.call-update) | async-done | bytes 655376 | tf_op jit(solution)/shard_map/reduce_scatter | solution.py:163
  707.5 54.6 %all-gather.20.cloned.1.call-done = bf16[640,2048]{1,0:T(8,128)(2,1)} async-done(((bf16[160,2048]{1,0:T(8,128)(2,1)}), bf16[640,2048]{1,0:T(8,128)(2,1)}) %all-gather.20.cloned.1.call-update) | async-done | bytes 2621456 | tf_op jit(solution)/shard_map/all_gather | solution.py:160
  762.1 11.7 fusion.128
  809.3 51.0 %reduce-scatter.11.cloned.1.call-done = bf16[160,2048]{1,0:T(8,128)(2,1)} async-done(((bf16[640,2048]{1,0:T(8,128)(2,1)}), bf16[160,2048]{1,0:T(8,128)(2,1)}) %reduce-scatter.11.cloned.1.call-update) | async-done | bytes 655376 | tf_op jit(solution)/shard_map/reduce_scatter | solution.py:163
  864.9 54.6 %all-gather.22.cloned.1.call-done = bf16[640,2048]{1,0:T(8,128)(2,1)} async-done(((bf16[160,2048]{1,0:T(8,128)(2,1)}), bf16[640,2048]{1,0:T(8,128)(2,1)}) %all-gather.22.cloned.1.call-update) | async-done | bytes 2621456 | tf_op jit(solution)/shard_map/all_gather | solution.py:160
  927.1 13.0 %all_to_all.87 = bf16[4,640,128]{2,1,0:T(8,128)(2,1)S(1)} all-to-all(bf16[4,640,128]{2,1,0:T(8,128)(2,1)S(1)} %bitcast.259), channel_id=1, replica_groups=mesh['dp'=2,'row'=4,'col'=4] {'row'}, dimensions={0} | all-to-all | bytes 1310720 | tf_op jit(solution)/shard_map/all_to_all | solution.py:173
  951.4 20.4 %multiply_reduce_fusion = (f32[2560]{0:T(1024)S(1)}, f32[2560,2560]{0,1:T(8,128)}) fusion(f32[2560]{0:T(1024)S(1)} %copy-done.62, f32[2560,2560]{0,1:T(8,128)} %copy-done.2, f32[2560]{0:T(1024)S(1)} %copy-done.60, bf16[2560,128]{1,0:T(8,128)(2,1)S(1)} %bitcast.276, bf16[2560,384]{1,0:T(8,128)(2,1)S(1)} %bitcast.252), kind=kOutput, calls=%fused_computation.1 | convolution fusion | flops 1703933440 | bytes 53774336 | tf_op jit(solution)/shard_map/dot_general | solution.py:35
  971.9 22.4 %multiply_convert_fusion = bf16[2560,2560]{0,1:T(8,128)(2,1)} fusion(f32[2560,2560]{0,1:T(8,128)} %get-tuple-element.100, f32[2560]{0:T(1024)S(1)} %get-tuple-element.99, f32[2560]{0:T(1024)S(1)} %copy-done.62, f32[2560,2560]{0,1:T(8,128)} %copy-done.2, f32[2560]{0:T(1024)S(1)} %copy-done.60), kind=kLoop, calls=%fused_computation | loop fusion | flops 32768000 | bytes 65566720 | tf_op jit(solution)/shard_map/convert_element_type | solution.py:274
  1026.0 17.8 %all-to-all-done.6 = bf16[4,640,384]{2,1,0:T(8,128)(2,1)S(1)} async-done(((bf16[4,640,384]{2,1,0:T(8,128)(2,1)}), bf16[4,640,384]{2,1,0:T(8,128)(2,1)S(1)}, u32[]{:S(2)}, u32[]{:S(2)}) %all-to-all-start.6) | async-done | bytes 1966112 | tf_op jit(solution)/shard_map/all_to_all | solution.py:186
  1121.8 12.4 all-reduce.7.cloned.1.call-done
  1135.1 36.2 %all-reduce.5.cloned.1.call-done = bf16[4,7,4,512]{3,2,0,1:T(4,128)(2,1)} async-done(((bf16[4,7,4,512]{3,2,0,1:T(4,128)(2,1)}), bf16[4,7,4,512]{3,2,0,1:T(4,128)(2,1)}) %all-reduce.5.cloned.1.call-update) | async-done | bytes 114704
  1184.1 41.5 %reduce-scatter.13.cloned.1.call-done = bf16[160,2048]{1,0:T(8,128)(2,1)} async-done(((bf16[640,2048]{1,0:T(8,128)(2,1)}), bf16[160,2048]{1,0:T(8,128)(2,1)}) %reduce-scatter.13.cloned.1.call-update) | async-done | bytes 655376 | tf_op jit(solution)/shard_map/reduce_scatter | solution.py:163
  (367 shorter events, 402.5 us)
Async XLA Ops:
  7.2 357.3 %copy-start = (f32[2,8,16,2048]{3,2,1,0:T(8,128)S(1)}, f32[2,8,16,2048]{3,2,1,0:T(8,128)}, u32[]{:S(2)}) copy-start(f32[2,8,16,2048]{3,2,1,0:T(8,128)} %param.41) | copy-start | bytes 6291460
  7.2 71.5 %all-gather.10.cloned.1.call-start = ((), (), s32[]{:S(2)}) async-start(), calls=%async_computation.13 | async-start | bytes 3276800 | tf_op jit(solution)/shard_map/all_gather | solution.py:160
  22.8 102.7 %all-gather.12.cloned.1.call-start = ((), (), s32[]{:S(2)}) async-start(), calls=%async_computation.14 | async-start | bytes 7864320 | tf_op jit(solution)/shard_map/all_gather | solution.py:146
  173.0 40.2 %all-to-all-start.1 = ((bf16[4,640,384]{1,2,0:T(8,128)(2,1)}), bf16[4,640,384]{1,2,0:T(8,128)(2,1)}, u32[]{:S(2)}, u32[]{:S(2)}) async-start(bf16[4,640,384]{1,2,0:T(8,128)(2,1)} %bitcast.245), calls=%async_computation.1 | async-start | bytes 3932160 | tf_op jit(solution)/shard_map/all_to_all | solution.py:173
  177.6 87.4 %all-gather.14.cloned.1.call-start = ((), (), s32[]{:S(2)}) async-start(), calls=%async_computation.15 | async-start | bytes 2621440 | tf_op jit(solution)/shard_map/all_gather | solution.py:149
  178.3 142.6 %reduce-scatter.7.cloned.1.call-start = ((), (), s32[]{:S(2)}) async-start(), calls=%async_computation.16 | async-start | bytes 3276800 | tf_op jit(solution)/shard_map/reduce_scatter | solution.py:163
  271.4 50.9 %copy-start.19 = (bf16[4,20,8,512]{3,2,0,1:T(8,128)(2,1)S(1)}, bf16[4,20,8,512]{3,2,0,1:T(8,128)(2,1)}, u32[]{:S(2)}) copy-start(bf16[4,20,8,512]{3,2,0,1:T(8,128)(2,1)} %copy.129) | copy-start | bytes 1966084
  271.4 332.4 %all-gather.16.cloned.1.call-start = ((), (), s32[]{:S(2)}) async-start(), calls=%async_computation.17 | async-start | bytes 3276800 | tf_op jit(solution)/shard_map/all_gather | solution.py:160
  271.5 53.1 %collective-permute-start = (bf16[512,2,2048]{2,1,0:T(2,128)(2,1)}, bf16[512,2,2048]{2,1,0:T(2,128)(2,1)}, u32[]{:S(2)}, u32[]{:S(2)}) collective-permute-start(bf16[512,2,2048]{2,1,0:T(2,128)(2,1)} %param.34), channel_id=1, source_target_pairs={{0,4},{4,0},{8,12},{12,8},{1,5},{5,1},{9,13},{13,9},{2,6},{6,2},{1... | collective-permute-start | bytes 12582920 | tf_op jit(solution)/shard_map/ppermute | solution.py:22
  324.5 314.6 %all-gather.18.cloned.1.call-start = ((), (), s32[]{:S(2)}) async-start(), calls=%async_computation.18 | async-start | bytes 10485760 | tf_op jit(solution)/shard_map/all_gather | solution.py:151
  345.7 227.3 %collective-permute-start.1 = (bf16[1024,2,2048]{2,1,0:T(2,128)(2,1)}, bf16[1024,2,2048]{2,1,0:T(2,128)(2,1)}, u32[]{:S(2)}, u32[]{:S(2)}) collective-permute-start(bf16[1024,2,2048]{2,1,0:T(2,128)(2,1)} %broadcast_select_fusion), channel_id=1, source_target_pairs={{0,8},{4,12},{8,0},{12,4},{1,9},{5,13},{9,1},{13,5},{2,10},{6,14},... | collective-permute-start | bytes 25165832 | tf_op jit(solution)/shard_map/ppermute | solution.py:22
  347.2 356.1 %reduce-scatter.9.cloned.1.call-start = ((), (), s32[]{:S(2)}) async-start(), calls=%async_computation.19 | async-start | bytes 3276800 | tf_op jit(solution)/shard_map/reduce_scatter | solution.py:163
  651.2 110.9 %all-gather.20.cloned.1.call-start = ((), (), s32[]{:S(2)}) async-start(), calls=%async_computation.20 | async-start | bytes 3276800 | tf_op jit(solution)/shard_map/all_gather | solution.py:160
  665.3 196.6 %copy-start.3 = (f32[4,20,8,512]{3,2,0,1:T(8,128)}, f32[4,20,8,512]{3,2,0,1:T(8,128)S(1)}, u32[]{:S(2)}) copy-start(f32[4,20,8,512]{3,2,0,1:T(8,128)S(1)} %copy.130) | copy-start | bytes 3932164
  707.4 152.9 %reduce-scatter.11.cloned.1.call-start = ((), (), s32[]{:S(2)}) async-start(), calls=%async_computation.21 | async-start | bytes 3276800 | tf_op jit(solution)/shard_map/reduce_scatter | solution.py:163
  809.3 51.1 %copy-start.20 = (bf16[160,2048]{1,0:T(8,128)(2,1)S(1)}, bf16[160,2048]{1,0:T(8,128)(2,1)}, u32[]{:S(2)}) copy-start(bf16[160,2048]{1,0:T(8,128)(2,1)} %reduce-scatter.7.cloned.1.call-done) | copy-start | bytes 1966084
  809.3 110.3 %all-gather.22.cloned.1.call-start = ((), (), s32[]{:S(2)}) async-start(), calls=%async_computation.22 | async-start | bytes 3276800 | tf_op jit(solution)/shard_map/all_gather | solution.py:160
  1015.7 28.0 %all-to-all-start.6 = ((bf16[4,640,384]{2,1,0:T(8,128)(2,1)}), bf16[4,640,384]{2,1,0:T(8,128)(2,1)S(1)}, u32[]{:S(2)}, u32[]{:S(2)}) async-start(bf16[4,640,384]{2,1,0:T(8,128)(2,1)} %bitcast.246), calls=%async_computation.9 | async-start | bytes 3932160 | tf_op jit(solution)/shard_map/all_to_all | solution.py:186
  1019.5 79.7 %reduce-scatter.15.cloned.1.call-start = ((), (), s32[]{:S(2)}) async-start(), calls=%async_computation.24 | async-start | bytes 573440 | tf_op jit(solution)/shard_map/reduce_scatter | solution.py:296
  1080.2 54.0 %all-reduce.7.cloned.1.call-start = ((), (), s32[]{:S(2)}) async-start(), calls=%async_computation.26 | async-start | bytes 524288
  1086.4 84.9 %all-reduce.5.cloned.1.call-start = ((), (), s32[]{:S(2)}) async-start(), calls=%async_computation.25 | async-start | bytes 229376
  1100.8 124.8 %reduce-scatter.13.cloned.1.call-start = ((), (), s32[]{:S(2)}) async-start(), calls=%async_computation.23 | async-start | bytes 3276800 | tf_op jit(solution)/shard_map/reduce_scatter | solution.py:163
  1107.7 14.1 %all-to-all-start.3 = ((bf16[160,4,512]{2,0,1:T(8,128)(2,1)}), bf16[160,4,512]{2,0,1:T(8,128)(2,1)S(1)}, u32[]{:S(2)}, u32[]{:S(2)}) async-start(bf16[160,4,512]{2,0,1:T(8,128)(2,1)} %bitcast.217), calls=%async_computation.5 | async-start | bytes 1310720 | tf_op jit(solution)/shard_map/all_to_all | solution.py:157
  1227.9 13.8 %all-to-all-start.7 = ((bf16[160,4,512]{2,0,1:T(8,128)(2,1)}), bf16[160,4,512]{2,0,1:T(8,128)(2,1)S(1)}, u32[]{:S(2)}, u32[]{:S(2)}) async-start(bf16[160,4,512]{2,0,1:T(8,128)(2,1)} %bitcast.216), calls=%async_computation.11 | async-start | bytes 1310720 | tf_op jit(solution)/shard_map/all_to_all | solution.py:157
  (78 other events, 723.8 us)
Sparse Core Ops, SparseCore 0:
  22.9 55.7 all-gather.9
  80.3 45.1 all-gather.11
  180.0 32.5 all-gather.13
  271.5 49.3 reduce-scatter.6
  324.6 54.4 all-gather.15
  380.6 102.1 all-gather.17
  651.3 51.9 reduce-scatter.8
  707.5 54.4 all-gather.19
  809.4 50.8 reduce-scatter.10
  865.0 54.4 all-gather.21
  1080.3 18.8 reduce-scatter.14
  1102.0 32.1 all-reduce.6
  1137.2 34.0 all-reduce.4
  1173.5 52.0 reduce-scatter.12
